TPU v7x, 128 devices: a whole 4x4x4 slice. The times are simulated.
128 devices in a mesh: wide: 32 (over y, z, core), narrow: 4 (over x).
Axes of the slice: x: 4, y: 4, z: 4, core: 2. Of those that a mesh axis runs over, the one named last changes fastest.
Arguments:
- layer_input_rows: bfloat16 [65536, 4096], P('wide', 'narrow'), may hold values from -6 to 6
- output_gradient_rows: bfloat16 [65536, 4096], P('wide', 'narrow'), may hold values from -60 to 60
- adapter_up_weight: bfloat16 [4096, 128], P('narrow'), may hold values from -0.09375 to 0.09375
- input_side_projection: bfloat16 [4096, 128], P('narrow'), may hold values from -0.09375 to 0.09375
- rank_side_projection: bfloat16 [128, 64], replicated, may hold values from -6 to 6
- lengths: int32 [2048], P('wide'), may hold values from 1 to 32, 40960 in all
- program_output_index: int32 [2048], replicated, may hold values from 0 to 2047, each once
- targets: bfloat16 [65536, 8192], P('wide', 'narrow'), may hold values from -650 to 650
Outputs:
- scores: float32 [2048, 65536], P('narrow', 'wide')
Inputs may be any that keep to these rules, and one draw needn't show every extreme that they name: Program s uses its first lengths[s] token rows; some program uses all 32. `program_output_index`: each output row is named by exactly one program.
All inputs are finite; a program needn't handle non-finite values. No bound on the sum of `lengths` on one device may be relied on, other than what follows from the above.
Results may differ from a plain program's by a relative error of at most 0.025.
Values may be sent and summed in bfloat16 or wider, within the bound.
A program may use at most 128 MiB of HBM per device.

v0:
```python
import math
import jax
import jax.numpy as jnp
from jax import lax
from jax.sharding import PartitionSpec as P

epsilon = 1e-06
SCORE_CHUNKS = 4


def program_features(out_side, in_side, lengths, length):
    programs = lengths.shape[0]
    positions = lax.broadcasted_iota(jnp.int32, (programs, length), 1)
    live_rows = (positions < lengths[:, None]).astype(jnp.float32)
    weighted = out_side.reshape(programs, length, -1) * live_rows[:, :, None]
    inputs = in_side.reshape(programs, length, -1)
    outer_sum = jnp.einsum("sla,slb->sab", weighted, inputs, precision=lax.Precision.HIGHEST)
    return outer_sum.reshape(programs, -1)


def normalize_rows(features, squares):
    return (features * lax.rsqrt(squares + epsilon)[:, None]).astype(jnp.bfloat16)


def narrow_sum(own, send_for, count, index, link_type=jnp.bfloat16):
    total = own
    for shift in range(1, count):
        perm = [(i, (i + shift) % count) for i in range(count)]
        piece = send_for((index + shift) % count).astype(link_type)
        total = total + lax.ppermute(piece, "narrow", perm).astype(jnp.float32)
    return total


def shards(
    layer_input_rows,
    output_gradient_rows,
    adapter_up_weight,
    input_side_projection,
    rank_side_projection,
    lengths,
    program_output_index,
    targets,
):
    narrow_count = lax.axis_size("narrow")
    narrow_index = lax.axis_index("narrow")
    programs = lengths.shape[0]
    length = layer_input_rows.shape[0] // programs
    target_wide = targets.astype(jnp.float32)
    target_squares = lax.psum(jnp.sum(target_wide * target_wide, axis=1), "narrow")
    reduced_sums = jnp.dot(
        output_gradient_rows, adapter_up_weight, preferred_element_type=jnp.float32
    )
    out_part = jnp.dot(
        reduced_sums, rank_side_projection.astype(jnp.float32), precision=lax.Precision.HIGHEST
    )
    in_part = jnp.dot(layer_input_rows, input_side_projection, preferred_element_type=jnp.float32)
    quarter_cols = out_part.shape[1] // narrow_count

    def send_for(dest):
        quarter = lax.dynamic_slice_in_dim(out_part, dest * quarter_cols, quarter_cols, 1)
        return jnp.concatenate([quarter, in_part], axis=1)

    summed_parts = narrow_sum(send_for(narrow_index), send_for, narrow_count, narrow_index)
    quarter = summed_parts[:, :quarter_cols]
    in_all = summed_parts[:, quarter_cols:]
    features = program_features(quarter, in_all, lengths, length)
    squares = jnp.sum(features * features, axis=1)
    squares = narrow_sum(squares, lambda dest: squares, narrow_count, narrow_index, jnp.float32)
    unit_rows = normalize_rows(features, squares)
    target_unit = normalize_rows(target_wide, target_squares)
    row_order = jnp.argsort(program_output_index)
    contract = (((1,), (1,)), ((), ()))
    root_count = math.sqrt(float(targets.shape[1] * narrow_count))
    gathered = lax.all_gather(unit_rows, "wide", axis=0, tiled=True)
    permuted = jnp.take(gathered, row_order, axis=0)
    chunk = target_unit.shape[0] // SCORE_CHUNKS
    pieces = []
    for c in range(SCORE_CHUNKS):
        part = lax.dot_general(
            permuted,
            target_unit[c * chunk : (c + 1) * chunk],
            contract,
            preferred_element_type=jnp.float32,
        ).astype(jnp.bfloat16)
        pieces.append(
            lax.psum_scatter(part, "narrow", scatter_dimension=0, tiled=True).astype(jnp.float32)
        )
    return jnp.concatenate(pieces, axis=1) * root_count


def solution(mesh):
    return jax.shard_map(
        shards,
        mesh=mesh,
        in_specs=(
            P("wide", "narrow"),
            P("wide", "narrow"),
            P("narrow", None),
            P("narrow", None),
            P(),
            P("wide"),
            P(),
            P("wide", "narrow"),
        ),
        out_specs=P("narrow", "wide"),
        check_vma=False,
    )
```

profile of v0, /device:TPU:1, one launch (start us, length us, event | category | flops | bytes accessed | tf_op | source)
XLA Modules:
  0.0 278.4 jit_solution(10977193983828737708)
XLA Ops:
  6.5 3.6 %fusion.14 = f32[2048,128]{1,0:T(8,128)S(1)} fusion(bf16[2048,1024]{1,0:T(8,128)(2,1)} %param.9, bf16[1024,128]{1,0:T(8,128)(2,1)} %param.10), kind=kOutput, calls=%fused_computation.39 | convolution fusion | flops 536870912 | bytes 5505024 | tf_op jit(solution)/shard_map/dot_general | solution.py:50
  11.0 1.5 fusion.13
  13.6 2.0 collective-permute-start
  15.6 2.5 collective-permute-start.1
  19.3 10.5 %collective-permute-done = bf16[2048,144]{0,1:T(8,128)(2,1)} collective-permute-done((bf16[2048,144]{0,1:T(8,128)(2,1)}, bf16[2048,144]{0,1:T(8,128)(2,1)}, u32[]{:S(2)}, u32[]{:S(2)}) %collective-permute-start) | collective-permute-done | bytes 589856 | tf_op jit(solution)/shard_map/ppermute | solution.py:30
  29.8 13.9 %collective-permute-done.1 = bf16[2048,144]{0,1:T(8,128)(2,1)} collective-permute-done((bf16[2048,144]{0,1:T(8,128)(2,1)S(1)}, bf16[2048,144]{0,1:T(8,128)(2,1)}, u32[]{:S(2)}, u32[]{:S(2)}) %collective-permute-start.1) | collective-permute-done | bytes 589856 | tf_op jit(solution)/shard_map/ppermute | solution.py:30
  43.8 1.7 fusion.7
  46.2 1.7 multiply_reduce_fusion
  48.7 3.0 %collective-permute-start.4 = (f32[64]{0:T(128)S(1)}, f32[64]{0:T(128)S(1)}, u32[]{:S(2)}, u32[]{:S(2)}) collective-permute-start(f32[64]{0:T(128)S(1)} %get-tuple-element.15), channel_id=1, source_target_pairs={{0,2},{1,3},{2,0},{3,1},{4,6},{5,7},{6,4},{7,5},{8,10},{9,11},{10,... | collective-permute-start | bytes 776 | tf_op jit(solution)/shard_map/ppermute | solution.py:30
  52.7 1.5 collective-permute-done.5
  55.2 5.0 %sort.17 = (s32[2048]{0:T(1024)}, s32[2048]{0:T(1024)S(1)}) sort(s32[2048]{0:T(1024)S(1)} %copy-done.4, s32[2048]{0:T(1024)S(1)} %iota.11), dimensions={0}, to_apply=%region_0.0 | sort | flops 22528 | bytes 32768 | tf_op jit(solution)/shard_map/jit(argsort)/sort | solution.py:71
  60.2 5.1 %fusion = f32[2048]{0:T(1024)S(1)} fusion(bf16[2048,2048]{1,0:T(8,128)(2,1)} %param.15), kind=kLoop, calls=%fused_computation.3 | loop fusion | flops 12580864 | bytes 8396800 | tf_op jit(solution)/shard_map/reduce_sum | solution.py:49
  65.3 7.6 %psum.7 = f32[2048]{0:T(1024)S(1)} all-reduce(f32[2048]{0:T(1024)S(1)} %fusion), channel_id=1, replica_groups=mesh['wide'=32,'narrow'=4] {'narrow'}, use_global_device_ids=true, to_apply=%region_3.4 | all-reduce | flops 2048 | bytes 16384 | tf_op jit(solution)/shard_map/psum | solution.py:49
  73.0 8.1 %fusion.1 = bf16[2048,2048]{1,0:T(8,128)(2,1)} fusion(bf16[2048,2048]{1,0:T(8,128)(2,1)} %param.15, f32[2048]{0:T(1024)S(1)} %add_rsqrt_fusion), kind=kLoop, calls=%fused_computation.4 | loop fusion | flops 12582912 | bytes 16785408 | tf_op jit(solution)/shard_map/convert_element_type | solution.py:22
  81.1 31.5 %all-gather.2.cloned.1.call-done = bf16[2048,2048]{1,0:T(8,128)(2,1)} async-done(((bf16[64,2048]{1,0:T(8,128)(2,1)}), bf16[2048,2048]{1,0:T(8,128)(2,1)}) %all-gather.2.cloned.1.call-update) | async-done | bytes 8388624 | tf_op jit(solution)/shard_map/all_gather | solution.py:74
  112.5 20.8 %gather_fusion = bf16[2048,2048]{1,0:T(8,128)(2,1)} fusion(bf16[2048,2048]{1,0:T(8,128)(2,1)} %all-gather.2.cloned.1.call-done, s32[2048]{0:T(1024)S(1)} %fusion.12), kind=kCustom, calls=%fused_computation | custom fusion | bytes 16785408 | tf_op jit(solution)/shard_map/jit(_take)/gather | solution.py:75
  133.3 10.1 %convolution_convert_fusion.3 = bf16[2048,512]{1,0:T(8,128)(2,1)} fusion(bf16[2048,2048]{1,0:T(8,128)(2,1)} %fusion.1, bf16[2048,2048]{1,0:T(8,128)(2,1)} %gather_fusion, pred[2048]{0:T(1024)(128)(4,1)S(1)} %compare_and_fusion), kind=kOutput, calls=%fused_computation.10 | convolution fusion | flops 4300210176 | bytes 12584960 | tf_op jit(solution)/shard_map/dot_general | solution.py:79
  143.7 10.1 %convolution_convert_fusion.2 = bf16[2048,512]{1,0:T(8,128)(2,1)} fusion(bf16[2048,2048]{1,0:T(8,128)(2,1)} %fusion.1, bf16[2048,2048]{1,0:T(8,128)(2,1)} %gather_fusion, pred[2048]{0:T(1024)(128)(4,1)S(1)} %compare_and_fusion), kind=kOutput, calls=%fused_computation.9 | convolution fusion | flops 4300210176 | bytes 12584960 | tf_op jit(solution)/shard_map/dot_general | solution.py:79
  153.9 10.1 %convolution_convert_fusion.1 = bf16[2048,512]{1,0:T(8,128)(2,1)} fusion(bf16[2048,2048]{1,0:T(8,128)(2,1)} %fusion.1, bf16[2048,2048]{1,0:T(8,128)(2,1)} %gather_fusion, pred[2048]{0:T(1024)(128)(4,1)S(1)} %compare_and_fusion), kind=kOutput, calls=%fused_computation.8 | convolution fusion | flops 4300210176 | bytes 12584960 | tf_op jit(solution)/shard_map/dot_general | solution.py:79
  164.4 10.1 %convolution_convert_fusion = bf16[2048,512]{1,0:T(8,128)(2,1)} fusion(bf16[2048,2048]{1,0:T(8,128)(2,1)} %fusion.1, bf16[2048,2048]{1,0:T(8,128)(2,1)} %gather_fusion, pred[2048]{0:T(1024)(128)(4,1)S(1)} %compare_and_fusion), kind=kOutput, calls=%fused_computation.7 | convolution fusion | flops 4300210176 | bytes 12584960 | tf_op jit(solution)/shard_map/dot_general | solution.py:79
  174.6 29.8 %reduce-scatter.7.cloned.1.call-done = bf16[512,512]{1,0:T(8,128)(2,1)} async-done(((bf16[2048,512]{1,0:T(8,128)(2,1)}), bf16[512,512]{1,0:T(8,128)(2,1)}) %reduce-scatter.7.cloned.1.call-update) | async-done | bytes 524304 | tf_op jit(solution)/shard_map/reduce_scatter | solution.py:86
  204.3 31.7 %reduce-scatter.9.cloned.1.call-done = bf16[512,512]{1,0:T(8,128)(2,1)} async-done(((bf16[2048,512]{1,0:T(8,128)(2,1)}), bf16[512,512]{1,0:T(8,128)(2,1)}) %reduce-scatter.9.cloned.1.call-update) | async-done | bytes 524304 | tf_op jit(solution)/shard_map/reduce_scatter | solution.py:86
  236.0 31.8 %reduce-scatter.11.cloned.1.call-done = bf16[512,512]{1,0:T(8,128)(2,1)} async-done(((bf16[2048,512]{1,0:T(8,128)(2,1)}), bf16[512,512]{1,0:T(8,128)(2,1)}) %reduce-scatter.11.cloned.1.call-update) | async-done | bytes 524304 | tf_op jit(solution)/shard_map/reduce_scatter | solution.py:86
  267.8 4.1 %convert_multiply_fusion.2 = f32[512,2048]{1,0:T(8,128)} fusion(bf16[512,512]{1,0:T(8,128)(2,1)} %reduce-scatter.11.cloned.1.call-done, bf16[512,512]{1,0:T(8,128)(2,1)} %reduce-scatter.9.cloned.1.call-done, bf16[512,512]{1,0:T(8,128)(2,1)} %reduce-scatter.7.cloned.1.call-done, bf16[512,512]{1,0:T(8,128)(2,1)} %reduce-scatter.5.cloned.1.call-done), kind=kLoop, calls=%fused_computation.6 | loop fusion | flops 9437184 | bytes 6291456 | tf_op jit(solution)/shard_map/mul | solution.py:88
  (45 shorter events, 7.1 us)
Async XLA Ops:
  6.5 4.4 %copy-start = (bf16[1024,128]{1,0:T(8,128)(2,1)S(1)}, bf16[1024,128]{1,0:T(8,128)(2,1)}, u32[]{:S(2)}) copy-start(bf16[1024,128]{1,0:T(8,128)(2,1)} %param.11) | copy-start | bytes 786436
  6.5 3.6 %copy-start.3 = (bf16[128,64]{0,1:T(8,128)(2,1)S(1)}, bf16[128,64]{0,1:T(8,128)(2,1)}, u32[]{:S(2)}) copy-start(bf16[128,64]{0,1:T(8,128)(2,1)} %param.12) | copy-start | bytes 49156
  6.5 106.0 %all-gather.2.cloned.1.call-start = ((), (), s32[]{:S(2)}) async-start(), calls=%async_computation.4 | async-start | bytes 8650752 | tf_op jit(solution)/shard_map/all_gather | solution.py:74
  6.5 4.4 %copy-start.2 = (bf16[2048,1024]{1,0:T(8,128)(2,1)S(1)}, bf16[2048,1024]{1,0:T(8,128)(2,1)}, u32[]{:S(2)}) copy-start(bf16[2048,1024]{1,0:T(8,128)(2,1)} %param.8) | copy-start | bytes 12582916
  11.0 8.3 %copy-start.5 = (s32[64]{0:T(128)S(1)}, s32[64]{0:T(128)}, u32[]{:S(2)}) copy-start(s32[64]{0:T(128)} %param.13) | copy-start | bytes 772
  13.6 16.2 %collective-permute-start = (bf16[2048,144]{0,1:T(8,128)(2,1)}, bf16[2048,144]{0,1:T(8,128)(2,1)}, u32[]{:S(2)}, u32[]{:S(2)}) collective-permute-start(bf16[2048,144]{0,1:T(8,128)(2,1)} %get-tuple-element.7), channel_id=1, source_target_pairs={{0,1},{1,2},{2,3},{3,0},{4,5},{5,6},{6,7},{7,4},{8,9},{9,10},{10,1... | collective-permute-start | bytes 1769480 | tf_op jit(solution)/shard_map/ppermute | solution.py:30
  15.6 28.1 %collective-permute-start.1 = (bf16[2048,144]{0,1:T(8,128)(2,1)S(1)}, bf16[2048,144]{0,1:T(8,128)(2,1)}, u32[]{:S(2)}, u32[]{:S(2)}) collective-permute-start(bf16[2048,144]{0,1:T(8,128)(2,1)S(1)} %get-tuple-element.8), channel_id=1, source_target_pairs={{0,2},{1,3},{2,0},{3,1},{4,6},{5,7},{6,4},{7,5},{8,10},{9,11},{10,... | collective-permute-start | bytes 1769480 | tf_op jit(solution)/shard_map/ppermute | solution.py:30
  18.1 25.7 %collective-permute-start.2 = (bf16[2048,144]{0,1:T(8,128)(2,1)S(1)}, bf16[2048,144]{0,1:T(8,128)(2,1)}, u32[]{:S(2)}, u32[]{:S(2)}) collective-permute-start(bf16[2048,144]{0,1:T(8,128)(2,1)S(1)} %get-tuple-element.9), channel_id=1, source_target_pairs={{0,3},{1,0},{2,1},{3,2},{4,7},{5,4},{6,5},{7,6},{8,11},{9,8},{10,9... | collective-permute-start | bytes 1769480 | tf_op jit(solution)/shard_map/ppermute | solution.py:30
  45.5 9.6 %copy-start.4 = (s32[2048]{0:T(1024)S(1)}, s32[2048]{0:T(1024)}, u32[]{:S(2)}) copy-start(s32[2048]{0:T(1024)} %param.14) | copy-start | bytes 24580
  47.9 4.0 %collective-permute-start.3 = (f32[64]{0:T(128)S(1)}, f32[64]{0:T(128)S(1)}, u32[]{:S(2)}, u32[]{:S(2)}) collective-permute-start(f32[64]{0:T(128)S(1)} %get-tuple-element.15), channel_id=1, source_target_pairs={{0,1},{1,2},{2,3},{3,0},{4,5},{5,6},{6,7},{7,4},{8,9},{9,10},{10,1... | collective-permute-start | bytes 776 | tf_op jit(solution)/shard_map/ppermute | solution.py:30
  48.7 4.0 %collective-permute-start.4 = (f32[64]{0:T(128)S(1)}, f32[64]{0:T(128)S(1)}, u32[]{:S(2)}, u32[]{:S(2)}) collective-permute-start(f32[64]{0:T(128)S(1)} %get-tuple-element.15), channel_id=1, source_target_pairs={{0,2},{1,3},{2,0},{3,1},{4,6},{5,7},{6,4},{7,5},{8,10},{9,11},{10,... | collective-permute-start | bytes 776 | tf_op jit(solution)/shard_map/ppermute | solution.py:30
  51.8 2.4 collective-permute-start.5
  55.1 119.5 %reduce-scatter.5.cloned.1.call-start = ((), (), s32[]{:S(2)}) async-start(), calls=%async_computation.5 | async-start | bytes 2621440 | tf_op jit(solution)/shard_map/reduce_scatter | solution.py:86
  143.5 60.9 %reduce-scatter.7.cloned.1.call-start = ((), (), s32[]{:S(2)}) async-start(), calls=%async_computation.6 | async-start | bytes 2621440 | tf_op jit(solution)/shard_map/reduce_scatter | solution.py:86
  153.9 82.2 %reduce-scatter.9.cloned.1.call-start = ((), (), s32[]{:S(2)}) async-start(), calls=%async_computation.7 | async-start | bytes 2621440 | tf_op jit(solution)/shard_map/reduce_scatter | solution.py:86
  164.1 103.8 %reduce-scatter.11.cloned.1.call-start = ((), (), s32[]{:S(2)}) async-start(), calls=%async_computation.8 | async-start | bytes 2621440 | tf_op jit(solution)/shard_map/reduce_scatter | solution.py:86
  174.5 97.4 %copy-start.1 = (bf16[1024,128]{1,0:T(8,128)(2,1)S(1)}, bf16[1024,128]{1,0:T(8,128)(2,1)}, u32[]{:S(2)}) copy-start(bf16[1024,128]{1,0:T(8,128)(2,1)} %param.11) | copy-start | bytes 786436
Sparse Core Ops, SparseCore 0:
  55.2 57.2 all-gather.1
  143.6 28.7 reduce-scatter.4
  174.9 29.3 reduce-scatter.6
  206.6 29.3 reduce-scatter.8
  238.4 29.3 reduce-scatter.10
where the time goes:
time: 279 us; the launch traced here: 278 us
  waiting for transfers between devices  152 us (54%)
  matrix products  48.1 us (17%)
  other arithmetic  26.1 us (9%)
  local copies, waits for them, and re-layouts  21.5 us (8%)
  between operations  13.3 us (5%)
  starting transfers between devices  10.3 us (4%)
  blocking collectives  7.64 us (3%)
    reduce_scatter x4, waiting for transfers between devices, shards(): lax.psum_scatter(part, 'narrow', scatter_dimension=0, tiled=True)  93.3 us
    dot_general x4, matrix products, shards(): lax.dot_general(permuted, target_unit[c * chunk:(c + 1) * chunk], contrac...  40.5 us
    all_gather x1, waiting for transfers between devices, shards(): gathered = lax.all_gather(unit_rows, 'wide', axis=0, tiled=True)  31.5 us
    ppermute x6, waiting for transfers between devices, narrow_sum(): total = total + lax.ppermute(piece, 'narrow', perm).astype(jnp.float32)  26.7 us
    gather x1, local copies, waits for them, and re-layouts, shards(): permuted = jnp.take(gathered, row_order, axis=0)  20.8 us
    ppermute x6, starting transfers between devices, narrow_sum(): total = total + lax.ppermute(piece, 'narrow', perm).astype(jnp.float32)  9.65 us
    convert_element_type x2, other arithmetic, normalize_rows(): (features * lax.rsqrt(squares + epsilon)[:, None]).astype(jnp.bfloat16)  9 us
    psum x1, blocking collectives, shards(): lax.psum(jnp.sum(target_wide * target_wide, axis=1), 'narrow')  7.64 us
  transfers between devices with their start and end apart: 11, of which 8 were waited for; matrix products, arithmetic and copies ran while one was open for 17% of the time, Pallas kernels for 0%

commit v1 on v0

--- a/solution.py
+++ b/solution.py
@@ -1,3 +1,4 @@
+import functools
 import math
 import jax
 import jax.numpy as jnp
@@ -6,6 +7,19 @@
 
 epsilon = 1e-06
 SCORE_CHUNKS = 4
+
+
+def mix_table(xs, device_axis):
+    base_arr = jnp.concatenate(
+        lax.all_to_all(
+            jnp.stack([xs for _ in range(lax.axis_size(device_axis))], axis=0), device_axis, 0, 0
+        ),
+        axis=0,
+    )
+    return base_arr
+
+
+_find_node = functools.partial(mix_table, device_axis="wide")
 
 
 def program_features(out_side, in_side, lengths, length):
@@ -71,7 +85,7 @@
     row_order = jnp.argsort(program_output_index)
     contract = (((1,), (1,)), ((), ()))
     root_count = math.sqrt(float(targets.shape[1] * narrow_count))
-    gathered = lax.all_gather(unit_rows, "wide", axis=0, tiled=True)
+    gathered = _find_node(unit_rows)
     permuted = jnp.take(gathered, row_order, axis=0)
     chunk = target_unit.shape[0] // SCORE_CHUNKS
     pieces = []

time: 279 us -> 360 us (1.29)
  waiting for transfers between devices: 152 us -> 216 us
  starting transfers between devices: 10.3 us -> 21 us
  local copies, waits for them, and re-layouts: 21.5 us -> 25.7 us
    all_to_all x0 -> x1, waiting for transfers between devices: none -> 80.7 us  [mix_table(): lax.all_to_all(jnp.stack([xs for _ in range(lax.axis_size(device_axis))],...]
    all_gather x1 -> x0, waiting for transfers between devices: 31.5 us -> none  [shards(): gathered = lax.all_gather(unit_rows, 'wide', axis=0, tiled=True)]
    reduce_scatter x4, waiting for transfers between devices: 93.3 us -> 109 us  [shards(): lax.psum_scatter(part, 'narrow', scatter_dimension=0, tiled=True)]
    all_to_all x0 -> x1, starting transfers between devices: none -> 10.7 us  [mix_table(): lax.all_to_all(jnp.stack([xs for _ in range(lax.axis_size(device_axis))],...]
    another operation x1 -> x2, local copies, waits for them, and re-layouts: 0.03 us -> 4.31 us  [the longest x1 4.28 us: mix_table(): jnp.stack([xs for _ in range(lax.axis_size(device_axis))], axis=0)]
  transfers between devices with their start and end apart: 11 -> 11, of which waited for: 8 -> 9; matrix products, arithmetic and copies ran while one was open for 17% -> 14% of each run, Pallas kernels for 0% -> 0%
where the time goes in v1:
time: 360 us
  waiting for transfers between devices  216 us (60%)
  matrix products  48.3 us (13%)
  local copies, waits for them, and re-layouts  25.7 us (7%)
  other arithmetic  25.3 us (7%)
  starting transfers between devices  21 us (6%)
  between operations  13.3 us (4%)
  blocking collectives  9.59 us (3%)
    reduce_scatter x4, waiting for transfers between devices, shards(): lax.psum_scatter(part, 'narrow', scatter_dimension=0, tiled=True)  109 us
    all_to_all x1, waiting for transfers between devices, mix_table(): lax.all_to_all(jnp.stack([xs for _ in range(lax.axis_size(device_axis))],...  80.7 us
    dot_general x4, matrix products, shards(): lax.dot_general(permuted, target_unit[c * chunk:(c + 1) * chunk], contrac...  40.7 us
    ppermute x6, waiting for transfers between devices, narrow_sum(): total = total + lax.ppermute(piece, 'narrow', perm).astype(jnp.float32)  26.7 us
    gather x1, local copies, waits for them, and re-layouts, shards(): permuted = jnp.take(gathered, row_order, axis=0)  20.8 us
    all_to_all x1, starting transfers between devices, mix_table(): lax.all_to_all(jnp.stack([xs for _ in range(lax.axis_size(device_axis))],...  10.7 us
    ppermute x6, starting transfers between devices, narrow_sum(): total = total + lax.ppermute(piece, 'narrow', perm).astype(jnp.float32)  9.66 us
    psum x1, blocking collectives, shards(): lax.psum(jnp.sum(target_wide * target_wide, axis=1), 'narrow')  9.59 us
  transfers between devices with their start and end apart: 11, of which 9 were waited for; matrix products, arithmetic and copies ran while one was open for 14% of the time, Pallas kernels for 0%

profile of v1, /device:TPU:1, one launch (start us, length us, event | category | flops | bytes accessed | tf_op | source)
XLA Modules:
  0.0 359.6 jit_solution(1097506254515160845)
XLA Ops:
  6.5 3.6 %fusion.14 = f32[2048,128]{1,0:T(8,128)S(1)} fusion(bf16[2048,1024]{1,0:T(8,128)(2,1)} %param.9, bf16[1024,128]{1,0:T(8,128)(2,1)} %param.10), kind=kOutput, calls=%fused_computation.39 | convolution fusion | flops 536870912 | bytes 5505024 | tf_op jit(solution)/shard_map/dot_general | solution.py:64
  13.6 2.0 collective-permute-start
  15.6 2.5 collective-permute-start.1
  19.3 10.5 %collective-permute-done = bf16[2048,144]{0,1:T(8,128)(2,1)} collective-permute-done((bf16[2048,144]{0,1:T(8,128)(2,1)}, bf16[2048,144]{0,1:T(8,128)(2,1)}, u32[]{:S(2)}, u32[]{:S(2)}) %collective-permute-start) | collective-permute-done | bytes 589856 | tf_op jit(solution)/shard_map/ppermute | solution.py:44
  29.8 14.0 %collective-permute-done.1 = bf16[2048,144]{0,1:T(8,128)(2,1)} collective-permute-done((bf16[2048,144]{0,1:T(8,128)(2,1)S(1)}, bf16[2048,144]{0,1:T(8,128)(2,1)}, u32[]{:S(2)}, u32[]{:S(2)}) %collective-permute-start.1) | collective-permute-done | bytes 589856 | tf_op jit(solution)/shard_map/ppermute | solution.py:44
  46.2 1.7 multiply_reduce_fusion
  48.7 3.0 collective-permute-start.4
  54.3 4.3 %stack.2 = bf16[32,64,2048]{2,1,0:T(8,128)(2,1)} broadcast(bf16[64,2048]{1,0:T(8,128)(2,1)S(1)} %fusion.8), dimensions={1,2} | broadcast | bytes 8650752 | tf_op jit(solution)/shard_map/stack | solution.py:15
  58.6 10.7 %all-to-all-start = ((bf16[32,64,2048]{2,1,0:T(8,128)(2,1)}), bf16[32,64,2048]{2,1,0:T(8,128)(2,1)}, u32[]{:S(2)}, u32[]{:S(2)}) async-start(bf16[32,64,2048]{2,1,0:T(8,128)(2,1)} %stack.2), calls=%async_computation | async-start | bytes 16777216 | tf_op jit(solution)/shard_map/all_to_all | solution.py:14
  69.4 5.0 %sort.17 = (s32[2048]{0:T(1024)}, s32[2048]{0:T(1024)S(1)}) sort(s32[2048]{0:T(1024)S(1)} %copy-done.4, s32[2048]{0:T(1024)S(1)} %iota.11), dimensions={0}, to_apply=%region_0.0 | sort | flops 22528 | bytes 32768 | tf_op jit(solution)/shard_map/jit(argsort)/sort | solution.py:85
  74.4 5.1 %fusion = f32[2048]{0:T(1024)S(1)} fusion(bf16[2048,2048]{1,0:T(8,128)(2,1)} %param.15), kind=kLoop, calls=%fused_computation.3 | loop fusion | flops 12580864 | bytes 8396800 | tf_op jit(solution)/shard_map/reduce_sum | solution.py:63
  79.5 9.6 %psum.7 = f32[2048]{0:T(1024)S(1)} all-reduce(f32[2048]{0:T(1024)S(1)} %fusion), channel_id=1, replica_groups=mesh['wide'=32,'narrow'=4] {'narrow'}, use_global_device_ids=true, to_apply=%region_3.4 | all-reduce | flops 2048 | bytes 16384 | tf_op jit(solution)/shard_map/psum | solution.py:63
  89.1 8.0 %fusion.1 = bf16[2048,2048]{1,0:T(8,128)(2,1)} fusion(bf16[2048,2048]{1,0:T(8,128)(2,1)} %param.15, f32[2048]{0:T(1024)S(1)} %add_rsqrt_fusion), kind=kLoop, calls=%fused_computation.4 | loop fusion | flops 12582912 | bytes 16785408 | tf_op jit(solution)/shard_map/convert_element_type | solution.py:36
  97.1 80.7 %all-to-all-done = bf16[32,64,2048]{2,1,0:T(8,128)(2,1)} async-done(((bf16[32,64,2048]{2,1,0:T(8,128)(2,1)}), bf16[32,64,2048]{2,1,0:T(8,128)(2,1)}, u32[]{:S(2)}, u32[]{:S(2)}) %all-to-all-start) | async-done | bytes 8388640 | tf_op jit(solution)/shard_map/all_to_all | solution.py:14
  177.8 20.8 %gather_fusion = bf16[2048,2048]{1,0:T(8,128)(2,1)} fusion(bf16[2048,2048]{1,0:T(8,128)(2,1)} %bitcast.1, s32[2048]{0:T(1024)S(1)} %fusion.12), kind=kCustom, calls=%fused_computation | custom fusion | bytes 16785408 | tf_op jit(solution)/shard_map/jit(_take)/gather | solution.py:89
  198.6 10.1 %convolution_convert_fusion.3 = bf16[2048,512]{1,0:T(8,128)(2,1)} fusion(bf16[2048,2048]{1,0:T(8,128)(2,1)} %fusion.1, bf16[2048,2048]{1,0:T(8,128)(2,1)} %gather_fusion, pred[2048]{0:T(1024)(128)(4,1)S(1)} %compare_and_fusion), kind=kOutput, calls=%fused_computation.10 | convolution fusion | flops 4300210176 | bytes 12584960 | tf_op jit(solution)/shard_map/dot_general | solution.py:93
  209.0 10.1 %convolution_convert_fusion.2 = bf16[2048,512]{1,0:T(8,128)(2,1)} fusion(bf16[2048,2048]{1,0:T(8,128)(2,1)} %fusion.1, bf16[2048,2048]{1,0:T(8,128)(2,1)} %gather_fusion, pred[2048]{0:T(1024)(128)(4,1)S(1)} %compare_and_fusion), kind=kOutput, calls=%fused_computation.9 | convolution fusion | flops 4300210176 | bytes 12584960 | tf_op jit(solution)/shard_map/dot_general | solution.py:93
  219.2 10.1 %convolution_convert_fusion.1 = bf16[2048,512]{1,0:T(8,128)(2,1)} fusion(bf16[2048,2048]{1,0:T(8,128)(2,1)} %fusion.1, bf16[2048,2048]{1,0:T(8,128)(2,1)} %gather_fusion, pred[2048]{0:T(1024)(128)(4,1)S(1)} %compare_and_fusion), kind=kOutput, calls=%fused_computation.8 | convolution fusion | flops 4300210176 | bytes 12584960 | tf_op jit(solution)/shard_map/dot_general | solution.py:93
  229.6 10.5 %convolution_convert_fusion = bf16[2048,512]{1,0:T(8,128)(2,1)} fusion(bf16[2048,2048]{1,0:T(8,128)(2,1)} %fusion.1, bf16[2048,2048]{1,0:T(8,128)(2,1)} %gather_fusion, pred[2048]{0:T(1024)(128)(4,1)S(1)} %compare_and_fusion), kind=kOutput, calls=%fused_computation.7 | convolution fusion | flops 4300210176 | bytes 12584960 | tf_op jit(solution)/shard_map/dot_general | solution.py:93
  240.1 13.3 %reduce-scatter.5.cloned.1.call-done = bf16[512,512]{1,0:T(8,128)(2,1)} async-done(((bf16[2048,512]{1,0:T(8,128)(2,1)}), bf16[512,512]{1,0:T(8,128)(2,1)}) %reduce-scatter.5.cloned.1.call-update) | async-done | bytes 524304 | tf_op jit(solution)/shard_map/reduce_scatter | solution.py:100
  253.4 32.0 %reduce-scatter.7.cloned.1.call-done = bf16[512,512]{1,0:T(8,128)(2,1)} async-done(((bf16[2048,512]{1,0:T(8,128)(2,1)}), bf16[512,512]{1,0:T(8,128)(2,1)}) %reduce-scatter.7.cloned.1.call-update) | async-done | bytes 524304 | tf_op jit(solution)/shard_map/reduce_scatter | solution.py:100
  285.4 31.8 %reduce-scatter.9.cloned.1.call-done = bf16[512,512]{1,0:T(8,128)(2,1)} async-done(((bf16[2048,512]{1,0:T(8,128)(2,1)}), bf16[512,512]{1,0:T(8,128)(2,1)}) %reduce-scatter.9.cloned.1.call-update) | async-done | bytes 524304 | tf_op jit(solution)/shard_map/reduce_scatter | solution.py:100
  317.2 31.8 %reduce-scatter.11.cloned.1.call-done = bf16[512,512]{1,0:T(8,128)(2,1)} async-done(((bf16[2048,512]{1,0:T(8,128)(2,1)}), bf16[512,512]{1,0:T(8,128)(2,1)}) %reduce-scatter.11.cloned.1.call-update) | async-done | bytes 524304 | tf_op jit(solution)/shard_map/reduce_scatter | solution.py:100
  349.0 4.1 %convert_multiply_fusion.2 = f32[512,2048]{1,0:T(8,128)} fusion(bf16[512,512]{1,0:T(8,128)(2,1)} %reduce-scatter.11.cloned.1.call-done, bf16[512,512]{1,0:T(8,128)(2,1)} %reduce-scatter.9.cloned.1.call-done, bf16[512,512]{1,0:T(8,128)(2,1)} %reduce-scatter.7.cloned.1.call-done, bf16[512,512]{1,0:T(8,128)(2,1)} %reduce-scatter.5.cloned.1.call-done), kind=kLoop, calls=%fused_computation.6 | loop fusion | flops 9437184 | bytes 6291456 | tf_op jit(solution)/shard_map/mul | solution.py:102
  (45 shorter events, 11.1 us)
Async XLA Ops:
  6.5 4.4 %copy-start = (bf16[1024,128]{1,0:T(8,128)(2,1)S(1)}, bf16[1024,128]{1,0:T(8,128)(2,1)}, u32[]{:S(2)}) copy-start(bf16[1024,128]{1,0:T(8,128)(2,1)} %param.11) | copy-start | bytes 786436
  6.5 3.6 %copy-start.3 = (bf16[128,64]{0,1:T(8,128)(2,1)S(1)}, bf16[128,64]{0,1:T(8,128)(2,1)}, u32[]{:S(2)}) copy-start(bf16[128,64]{0,1:T(8,128)(2,1)} %param.12) | copy-start | bytes 49156
  6.5 4.4 %copy-start.2 = (bf16[2048,1024]{1,0:T(8,128)(2,1)S(1)}, bf16[2048,1024]{1,0:T(8,128)(2,1)}, u32[]{:S(2)}) copy-start(bf16[2048,1024]{1,0:T(8,128)(2,1)} %param.8) | copy-start | bytes 12582916
  10.9 8.3 %copy-start.5 = (s32[64]{0:T(128)S(1)}, s32[64]{0:T(128)}, u32[]{:S(2)}) copy-start(s32[64]{0:T(128)} %param.13) | copy-start | bytes 772
  13.6 16.2 %collective-permute-start = (bf16[2048,144]{0,1:T(8,128)(2,1)}, bf16[2048,144]{0,1:T(8,128)(2,1)}, u32[]{:S(2)}, u32[]{:S(2)}) collective-permute-start(bf16[2048,144]{0,1:T(8,128)(2,1)} %get-tuple-element.7), channel_id=1, source_target_pairs={{0,1},{1,2},{2,3},{3,0},{4,5},{5,6},{6,7},{7,4},{8,9},{9,10},{10,1... | collective-permute-start | bytes 1769480 | tf_op jit(solution)/shard_map/ppermute | solution.py:44
  15.6 28.1 %collective-permute-start.1 = (bf16[2048,144]{0,1:T(8,128)(2,1)S(1)}, bf16[2048,144]{0,1:T(8,128)(2,1)}, u32[]{:S(2)}, u32[]{:S(2)}) collective-permute-start(bf16[2048,144]{0,1:T(8,128)(2,1)S(1)} %get-tuple-element.8), channel_id=1, source_target_pairs={{0,2},{1,3},{2,0},{3,1},{4,6},{5,7},{6,4},{7,5},{8,10},{9,11},{10,... | collective-permute-start | bytes 1769480 | tf_op jit(solution)/shard_map/ppermute | solution.py:44
  18.1 25.7 %collective-permute-start.2 = (bf16[2048,144]{0,1:T(8,128)(2,1)S(1)}, bf16[2048,144]{0,1:T(8,128)(2,1)}, u32[]{:S(2)}, u32[]{:S(2)}) collective-permute-start(bf16[2048,144]{0,1:T(8,128)(2,1)S(1)} %get-tuple-element.9), channel_id=1, source_target_pairs={{0,3},{1,0},{2,1},{3,2},{4,7},{5,4},{6,5},{7,6},{8,11},{9,8},{10,9... | collective-permute-start | bytes 1769480 | tf_op jit(solution)/shard_map/ppermute | solution.py:44
  47.9 4.0 %collective-permute-start.3 = (f32[64]{0:T(128)S(1)}, f32[64]{0:T(128)S(1)}, u32[]{:S(2)}, u32[]{:S(2)}) collective-permute-start(f32[64]{0:T(128)S(1)} %get-tuple-element.15), channel_id=1, source_target_pairs={{0,1},{1,2},{2,3},{3,0},{4,5},{5,6},{6,7},{7,4},{8,9},{9,10},{10,1... | collective-permute-start | bytes 776 | tf_op jit(solution)/shard_map/ppermute | solution.py:44
  48.7 4.0 %collective-permute-start.4 = (f32[64]{0:T(128)S(1)}, f32[64]{0:T(128)S(1)}, u32[]{:S(2)}, u32[]{:S(2)}) collective-permute-start(f32[64]{0:T(128)S(1)} %get-tuple-element.15), channel_id=1, source_target_pairs={{0,2},{1,3},{2,0},{3,1},{4,6},{5,7},{6,4},{7,5},{8,10},{9,11},{10,... | collective-permute-start | bytes 776 | tf_op jit(solution)/shard_map/ppermute | solution.py:44
  51.8 2.4 collective-permute-start.5
  58.6 10.7 %copy-start.4 = (s32[2048]{0:T(1024)S(1)}, s32[2048]{0:T(1024)}, u32[]{:S(2)}) copy-start(s32[2048]{0:T(1024)} %param.14) | copy-start | bytes 24580
  58.6 119.2 %all-to-all-start = ((bf16[32,64,2048]{2,1,0:T(8,128)(2,1)}), bf16[32,64,2048]{2,1,0:T(8,128)(2,1)}, u32[]{:S(2)}, u32[]{:S(2)}) async-start(bf16[32,64,2048]{2,1,0:T(8,128)(2,1)} %stack.2), calls=%async_computation | async-start | bytes 16777216 | tf_op jit(solution)/shard_map/all_to_all | solution.py:14
  69.3 184.1 %reduce-scatter.5.cloned.1.call-start = ((), (), s32[]{:S(2)}) async-start(), calls=%async_computation.5 | async-start | bytes 2621440 | tf_op jit(solution)/shard_map/reduce_scatter | solution.py:100
  208.8 76.6 %reduce-scatter.7.cloned.1.call-start = ((), (), s32[]{:S(2)}) async-start(), calls=%async_computation.6 | async-start | bytes 2621440 | tf_op jit(solution)/shard_map/reduce_scatter | solution.py:100
  219.1 98.1 %reduce-scatter.9.cloned.1.call-start = ((), (), s32[]{:S(2)}) async-start(), calls=%async_computation.7 | async-start | bytes 2621440 | tf_op jit(solution)/shard_map/reduce_scatter | solution.py:100
  229.3 119.7 %reduce-scatter.11.cloned.1.call-start = ((), (), s32[]{:S(2)}) async-start(), calls=%async_computation.8 | async-start | bytes 2621440 | tf_op jit(solution)/shard_map/reduce_scatter | solution.py:100
  240.1 113.1 %copy-start.1 = (bf16[1024,128]{1,0:T(8,128)(2,1)S(1)}, bf16[1024,128]{1,0:T(8,128)(2,1)}, u32[]{:S(2)}) copy-start(bf16[1024,128]{1,0:T(8,128)(2,1)} %param.11) | copy-start | bytes 786436
Sparse Core Ops, SparseCore 0:
  208.9 44.4 reduce-scatter.4
  255.9 29.3 reduce-scatter.6
  287.8 29.3 reduce-scatter.8
  319.6 29.3 reduce-scatter.10
